TPU v7x, 128 devices: a whole 4x4x4 slice. The times are simulated.
128 devices in a mesh: grp: 8 (over x_hi, y), dom: 16 (over z, x_lo, core).
Axes of the slice: x: 4 (x_hi: 2, x_lo: 2; x = x_hi * 2 + x_lo), y: 4, z: 4, core: 2. Of those that a mesh axis runs over, the one named last changes fastest.
Arguments:
- features: bfloat16 [65536, 1024], P(('grp', 'dom')), may hold values from -6 to 6
- node_order: int32 [65536], P(('grp', 'dom')), may hold values from 0 to 65535, as said below
- block_cols: int32 [512, 16], P(('grp', 'dom')), may hold values from 0 to 63
- block_count: int32 [512], P(('grp', 'dom')), may hold values from 1 to 16, as said below
- block_vals: bfloat16 [512, 16, 128, 128], P(('grp', 'dom')), may hold values from -0.1875 to 0.1875
- weight: bfloat16 [1024, 512], replicated, may hold values from -0.1875 to 0.1875
- cotangent: bfloat16 [65536, 512], P(('grp', 'dom')), may hold values from -12 to 12
Outputs:
- hidden: bfloat16 [65536, 512], P(('grp', 'dom'))
- grad_weight: float32 [1024, 512], replicated
Inputs may be any that keep to these rules, and one draw needn't show every extreme that they name: `node_order`: A permutation of the crawl rows; the positions of one device's block of 512 take exactly 4 crawl rows from each device's block of 512 crawl rows. `block_count`: some row of blocks holds exactly 16 live blocks.
All inputs are finite; a program needn't handle non-finite values.
Results may differ from a plain program's by a relative error of at most 0.014.
Values may be sent and summed in bfloat16 or wider, within the bound.
A program may use at most 128 MiB of HBM per device.

v0:
```python
import jax
import jax.numpy as jnp
from jax import lax
from jax.sharding import PartitionSpec as P


def silu_slope(values):
    sig = jax.nn.sigmoid(values)
    return sig * (1.0 + values * (1.0 - sig))


def regroup(features, node_order):
    row_count, width_in = features.shape
    devices = lax.axis_size("grp") * lax.axis_size("dom")
    per_pair = row_count // devices
    source_device = node_order // row_count
    source_row = node_order % row_count
    ordering = jnp.argsort(source_device, stable=True)
    requests = source_row[ordering].reshape(devices, per_pair)
    asked_rows = lax.all_to_all(requests, ("grp", "dom"), split_axis=0, concat_axis=0, tiled=True)
    outgoing = features[asked_rows.reshape(-1)].reshape(devices, per_pair, width_in)
    arrived = lax.all_to_all(outgoing, ("grp", "dom"), split_axis=0, concat_axis=0, tiled=True)
    arrived = arrived.reshape(row_count, width_in)
    inverse = jnp.argsort(ordering)
    return arrived[inverse]


def shards(features, node_order, block_cols, block_count, block_vals, weight, cotangent):
    row_count, width_in = features.shape
    hidden_units = weight.shape[1]
    tiles_dev, blocks, tile_size, _ = block_vals.shape
    ordered = regroup(features, node_order)
    everyone = lax.all_gather(ordered, "dom", axis=0, tiled=True)
    panel_tiles = everyone.reshape(-1, tile_size, width_in)
    live_mask = lax.broadcasted_iota(jnp.int32, (tiles_dev, blocks), 1) < block_count[:, None]
    masked_vals = jnp.where(live_mask[:, :, None, None], block_vals, jnp.zeros((), jnp.bfloat16))
    selected = panel_tiles[block_cols]
    mixed = jnp.einsum("tkij,tkjf->tif", masked_vals, selected, preferred_element_type=jnp.float32)
    mixed = mixed.astype(jnp.bfloat16).reshape(row_count, width_in)
    aggregate = jnp.dot(mixed, weight, preferred_element_type=jnp.float32)
    hidden = jax.nn.silu(aggregate).astype(jnp.bfloat16)
    grad_agg = (cotangent.astype(jnp.float32) * silu_slope(aggregate)).astype(jnp.bfloat16)
    local_grad = lax.dot_general(
        mixed, grad_agg, (((0,), (0,)), ((), ())), preferred_element_type=jnp.float32
    )
    grad_weight = lax.psum(local_grad, ("grp", "dom"))
    return (hidden, grad_weight)


def solution(mesh):
    placed = (
        P(("grp", "dom"), None),
        P(("grp", "dom")),
        P(("grp", "dom"), None),
        P(("grp", "dom")),
        P(("grp", "dom"), None, None, None),
        P(),
        P(("grp", "dom"), None),
    )
    return jax.shard_map(
        shards,
        mesh=mesh,
        in_specs=placed,
        out_specs=(P(("grp", "dom"), None), P()),
        check_vma=False,
    )
```

profile of v0, /device:TPU:1, one launch (start us, length us, event | category | flops | bytes accessed | tf_op | source)
XLA Modules:
  0.0 341.9 jit_solution(17413993428679002675)
XLA Ops:
  7.2 0.8 add_select_fusion
  8.0 3.8 %sort.34 = (s32[512]{0:T(512)}, s32[512]{0:T(512)S(1)}) sort(s32[512]{0:T(512)S(1)} %get-tuple-element.6, s32[512]{0:T(512)S(1)} %iota.16), dimensions={0}, to_apply=%region_0.1 | sort | flops 4608 | bytes 8192 | tf_op jit(solution)/shard_map/jit(argsort)/sort | solution.py:18
  11.7 3.5 %gather_fusion = s32[512]{0:T(512)S(1)} fusion(s32[512]{0:T(512)S(1)} %get-tuple-element.7, s32[1024]{0:T(1024)S(1)} %pad_clamp_fusion.3), kind=kCustom, calls=%fused_computation | custom fusion | bytes 6144 | tf_op jit(solution)/shard_map/gather | solution.py:19
  15.2 0.1 all_to_all.9
  15.4 20.9 %all_to_all.14 = s32[128,1,4]{2,1,0:T(1,128)S(1)} all-to-all(s32[128,1,4]{2,1,0:T(1,128)S(1)} %bitcast.16), channel_id=1, replica_groups=mesh['grp'=8,'dom'=16] {'grp','dom'}, dimensions={0} | all-to-all | bytes 4096 | tf_op jit(solution)/shard_map/all_to_all | solution.py:20
  36.2 0.5 broadcast.76
  36.7 0.8 reduce.3
  37.6 0.1 reshape.71
  37.7 2.1 gather_fusion.1
  39.8 1.2 reshape.72
  41.0 4.4 %all-to-all-start.1 = ((bf16[128,4,1024]{2,1,0:T(4,128)(2,1)}), bf16[128,4,1024]{2,1,0:T(4,128)(2,1)S(1)}, u32[]{:S(2)}, u32[]{:S(2)}) async-start(bf16[128,4,1024]{2,1,0:T(4,128)(2,1)} %reshape.72), calls=%async_computation.1 | async-start | bytes 2097152 | tf_op jit(solution)/shard_map/all_to_all | solution.py:22
  45.4 3.8 %sort.35 = (s32[512]{0:T(512)}, s32[512]{0:T(512)S(1)}) sort(s32[512]{0:T(512)S(1)} %get-tuple-element.4, s32[512]{0:T(512)S(1)} %iota.17), dimensions={0}, to_apply=%region_1.2 | sort | flops 4608 | bytes 8192 | tf_op jit(solution)/shard_map/jit(argsort)/sort | solution.py:24
  49.2 15.2 %all-to-all-done.1 = bf16[128,4,1024]{2,1,0:T(4,128)(2,1)S(1)} async-done(((bf16[128,4,1024]{2,1,0:T(4,128)(2,1)}), bf16[128,4,1024]{2,1,0:T(4,128)(2,1)S(1)}, u32[]{:S(2)}, u32[]{:S(2)}) %all-to-all-start.1) | async-done | bytes 1048608 | tf_op jit(solution)/shard_map/all_to_all | solution.py:22
  64.4 0.3 reshape.73
  64.7 2.8 gather_fusion.2
  67.6 0.1 reshape.102
  67.7 0.1 iota_compare_fusion
  67.8 88.4 %all-gather.3.cloned.1.call-done = bf16[8192,1024]{1,0:T(8,128)(2,1)} async-done(((bf16[512,1024]{1,0:T(8,128)(2,1)}), bf16[8192,1024]{1,0:T(8,128)(2,1)}) %all-gather.3.cloned.1.call-update) | async-done | bytes 16777232 | tf_op jit(solution)/shard_map/all_gather | solution.py:33
  156.2 13.5 %gather_fusion.3 = bf16[64,128,1024]{2,1,0:T(8,128)(2,1)} fusion(bf16[64,128,1024]{2,1,0:T(8,128)(2,1)} %bitcast.13, s32[1024]{0:T(1024)S(1)} %pad_clamp_fusion), kind=kCustom, calls=%fused_computation.3 | custom fusion | bytes 33554688 | tf_op jit(solution)/shard_map/gather | solution.py:37
  169.7 7.3 %bitcast_convert_fusion = bf16[4,128,1024]{2,1,0:T(8,128)(2,1)S(1)} fusion(bf16[4,16,128,1024]{3,2,1,0:T(8,128)(2,1)} %bitcast.12, bf16[4,16,128,128]{3,2,1,0:T(8,128)(2,1)S(1)} %copy-done.1, pred[4,16]{1,0:T(4,128)(4,1)S(1)} %iota_compare_fusion), kind=kOutput, calls=%fused_computation.4 | convolution fusion | flops 2149056512 | bytes 19923008 | tf_op jit(solution)/shard_map/tkij,tkjf->tif/dot_general | solution.py:38
  177.0 1.6 multiply_convert_fusion.1
  178.7 2.2 fusion.6
  180.9 151.1 %all-reduce.2.cloned.1.call-done = f32[1024,512]{1,0:T(8,128)} async-done(((f32[1024,512]{1,0:T(8,128)}), f32[1024,512]{1,0:T(8,128)}) %all-reduce.2.cloned.1.call-update) | async-done | bytes 2097168 | tf_op jit(solution)/shard_map/psum | solution.py:46
  332.0 3.1 copy.12
  (26 shorter events, 0.2 us)
Async XLA Ops:
  7.2 30.5 %copy-start = (bf16[512,1024]{1,0:T(8,128)(2,1)S(1)}, bf16[512,1024]{1,0:T(8,128)(2,1)}, u32[]{:S(2)}) copy-start(bf16[512,1024]{1,0:T(8,128)(2,1)} %param.7) | copy-start | bytes 3145732
  41.0 23.5 %all-to-all-start.1 = ((bf16[128,4,1024]{2,1,0:T(4,128)(2,1)}), bf16[128,4,1024]{2,1,0:T(4,128)(2,1)S(1)}, u32[]{:S(2)}, u32[]{:S(2)}) async-start(bf16[128,4,1024]{2,1,0:T(4,128)(2,1)} %reshape.72), calls=%async_computation.1 | async-start | bytes 2097152 | tf_op jit(solution)/shard_map/all_to_all | solution.py:22
  45.4 110.8 %all-gather.3.cloned.1.call-start = ((), (), s32[]{:S(2)}) async-start(), calls=%async_computation.3 | async-start | bytes 17825792 | tf_op jit(solution)/shard_map/all_gather | solution.py:33
  64.7 2.9 copy-start.2
  64.7 3.0 copy-start.5
  67.5 264.5 %all-reduce.2.cloned.1.call-start = ((), (), s32[]{:S(2)}) async-start(), calls=%async_computation.2 | async-start | bytes 4194304 | tf_op jit(solution)/shard_map/psum | solution.py:46
  156.2 13.5 %copy-start.1 = (bf16[4,16,128,128]{3,2,1,0:T(8,128)(2,1)S(1)}, bf16[4,16,128,128]{3,2,1,0:T(8,128)(2,1)}, u32[]{:S(2)}) copy-start(bf16[4,16,128,128]{3,2,1,0:T(8,128)(2,1)} %param.11) | copy-start | bytes 6291460
  169.7 7.3 %copy-start.3 = (bf16[1024,512]{1,0:T(8,128)(2,1)S(1)}, bf16[1024,512]{1,0:T(8,128)(2,1)}, u32[]{:S(2)}) copy-start(bf16[1024,512]{1,0:T(8,128)(2,1)} %param.12) | copy-start | bytes 3145732
  177.0 1.7 copy-start.4
Sparse Core Ops, SparseCore 0:
  67.6 88.4 all-gather.2
  181.1 150.8 all-reduce.1
where the time goes:
time: 342 us
  waiting for transfers between devices  255 us (75%)
  local copies, waits for them, and re-layouts  27.2 us (8%)
  blocking collectives  20.9 us (6%)
  between operations  14.2 us (4%)
  matrix products  11.2 us (3%)
  other arithmetic  9.24 us (3%)
  starting transfers between devices  4.48 us (1%)
    psum x1, waiting for transfers between devices, shards(): grad_weight = lax.psum(local_grad, ('grp', 'dom'))  151 us
    all_gather x1, waiting for transfers between devices, shards(): everyone = lax.all_gather(ordered, 'dom', axis=0, tiled=True)  88.4 us
    all_to_all x1, blocking collectives, regroup(): lax.all_to_all(requests, ('grp', 'dom'), split_axis=0, concat_axis=0, til...  20.9 us
    all_to_all x1, waiting for transfers between devices, regroup(): lax.all_to_all(outgoing, ('grp', 'dom'), split_axis=0, concat_axis=0, til...  15.2 us
    gather x1, local copies, waits for them, and re-layouts, shards(): selected = panel_tiles[block_cols]  13.5 us
    dot_general x1, matrix products, shards(): jnp.einsum('tkij,tkjf->tif', masked_vals, selected, preferred_element_typ...  7.32 us
  transfers between devices with their start and end apart: 3, of which 3 were waited for; matrix products, arithmetic and copies ran while one was open for 1% of the time, Pallas kernels for 0%

commit v1 on v0

--- a/solution.py
+++ b/solution.py
@@ -2,6 +2,7 @@
 import jax.numpy as jnp
 from jax import lax
 from jax.sharding import PartitionSpec as P
+from jax.lax import psum
 
 
 def silu_slope(values):
@@ -43,7 +44,7 @@
     local_grad = lax.dot_general(
         mixed, grad_agg, (((0,), (0,)), ((), ())), preferred_element_type=jnp.float32
     )
-    grad_weight = lax.psum(local_grad, ("grp", "dom"))
+    grad_weight = psum(psum(local_grad, "dom"), "grp")
     return (hidden, grad_weight)
 
 

time: 342 us -> 411 us (1.20)
  waiting for transfers between devices: 255 us -> 320 us
    psum x1 -> x2, waiting for transfers between devices: 151 us -> 216 us  [shards(): grad_weight = psum(psum(local_grad, 'dom'), 'grp')]
  transfers between devices with their start and end apart: 3 -> 4, of which waited for: 3 -> 4; matrix products, arithmetic and copies ran while one was open for 1% -> 1% of each run, Pallas kernels for 0% -> 0%
where the time goes in v1:
time: 411 us; the launch traced here: 407 us
  waiting for transfers between devices  320 us (78%)
  local copies, waits for them, and re-layouts  27.2 us (7%)
  blocking collectives  20.9 us (5%)
  between operations  13.9 us (3%)
  matrix products  11.2 us (3%)
  other arithmetic  9.24 us (2%)
  starting transfers between devices  4.52 us (1%)
    psum x2, waiting for transfers between devices, shards(): grad_weight = psum(psum(local_grad, 'dom'), 'grp')  216 us
    all_gather x1, waiting for transfers between devices, shards(): everyone = lax.all_gather(ordered, 'dom', axis=0, tiled=True)  88.4 us
    all_to_all x1, blocking collectives, regroup(): lax.all_to_all(requests, ('grp', 'dom'), split_axis=0, concat_axis=0, til...  20.9 us
    all_to_all x1, waiting for transfers between devices, regroup(): lax.all_to_all(outgoing, ('grp', 'dom'), split_axis=0, concat_axis=0, til...  15.2 us
    gather x1, local copies, waits for them, and re-layouts, shards(): selected = panel_tiles[block_cols]  13.5 us
  transfers between devices with their start and end apart: 4, of which 4 were waited for; matrix products, arithmetic and copies ran while one was open for 1% of the time, Pallas kernels for 0%

profile of v1, /device:TPU:1, one launch (start us, length us, event | category | flops | bytes accessed | tf_op | source)
XLA Modules:
  0.0 406.8 jit_solution(1505442137292094990)
XLA Ops:
  7.2 0.8 add_select_fusion
  8.0 3.8 sort.34
  11.7 3.5 gather_fusion
  15.2 0.1 all_to_all.9
  15.4 20.9 %all_to_all.14 = s32[128,1,4]{2,1,0:T(1,128)S(1)} all-to-all(s32[128,1,4]{2,1,0:T(1,128)S(1)} %bitcast.16), channel_id=1, replica_groups=mesh['grp'=8,'dom'=16] {'grp','dom'}, dimensions={0} | all-to-all | bytes 4096 | tf_op jit(solution)/shard_map/all_to_all | solution.py:21
  36.2 0.5 broadcast.76
  36.7 0.8 reduce.3
  37.6 0.1 reshape.71
  37.7 2.1 gather_fusion.1
  39.8 1.2 reshape.72
  41.0 4.4 %all-to-all-start.1 = ((bf16[128,4,1024]{2,1,0:T(4,128)(2,1)}), bf16[128,4,1024]{2,1,0:T(4,128)(2,1)S(1)}, u32[]{:S(2)}, u32[]{:S(2)}) async-start(bf16[128,4,1024]{2,1,0:T(4,128)(2,1)} %reshape.72), calls=%async_computation.1 | async-start | bytes 2097152 | tf_op jit(solution)/shard_map/all_to_all | solution.py:23
  45.4 3.8 sort.35
  49.2 15.2 %all-to-all-done.1 = bf16[128,4,1024]{2,1,0:T(4,128)(2,1)S(1)} async-done(((bf16[128,4,1024]{2,1,0:T(4,128)(2,1)}), bf16[128,4,1024]{2,1,0:T(4,128)(2,1)S(1)}, u32[]{:S(2)}, u32[]{:S(2)}) %all-to-all-start.1) | async-done | bytes 1048608 | tf_op jit(solution)/shard_map/all_to_all | solution.py:23
  64.4 0.3 reshape.73
  64.7 2.8 gather_fusion.2
  67.6 0.1 reshape.102
  67.8 88.4 %all-gather.3.cloned.1.call-done = bf16[8192,1024]{1,0:T(8,128)(2,1)} async-done(((bf16[512,1024]{1,0:T(8,128)(2,1)}), bf16[8192,1024]{1,0:T(8,128)(2,1)}) %all-gather.3.cloned.1.call-update) | async-done | bytes 16777232 | tf_op jit(solution)/shard_map/all_gather | solution.py:34
  156.2 13.5 %gather_fusion.3 = bf16[64,128,1024]{2,1,0:T(8,128)(2,1)} fusion(bf16[64,128,1024]{2,1,0:T(8,128)(2,1)} %bitcast.13, s32[1024]{0:T(1024)S(1)} %pad_clamp_fusion), kind=kCustom, calls=%fused_computation.3 | custom fusion | bytes 33554688 | tf_op jit(solution)/shard_map/gather | solution.py:38
  169.7 7.3 %bitcast_convert_fusion = bf16[4,128,1024]{2,1,0:T(8,128)(2,1)S(1)} fusion(bf16[4,16,128,1024]{3,2,1,0:T(8,128)(2,1)} %bitcast.12, bf16[4,16,128,128]{3,2,1,0:T(8,128)(2,1)S(1)} %copy-done.1, pred[4,16]{1,0:T(4,128)(4,1)S(1)} %iota_compare_fusion), kind=kOutput, calls=%fused_computation.4 | convolution fusion | flops 2149056512 | bytes 19923008 | tf_op jit(solution)/shard_map/tkij,tkjf->tif/dot_general | solution.py:39
  177.0 1.6 multiply_convert_fusion.1
  178.7 2.2 fusion.6
  181.0 125.0 %all-reduce.3.cloned.1.call-done = f32[1024,512]{1,0:T(8,128)} async-done(((f32[1024,512]{1,0:T(8,128)}), f32[1024,512]{1,0:T(8,128)}) %all-reduce.3.cloned.1.call-update) | async-done | bytes 2097168 | tf_op jit(solution)/shard_map/psum | solution.py:47
  306.0 91.2 %all-reduce.5.cloned.1.call-done = f32[1024,512]{1,0:T(8,128)} async-done(((f32[1024,512]{1,0:T(8,128)}), f32[1024,512]{1,0:T(8,128)}) %all-reduce.5.cloned.1.call-update) | async-done | bytes 2097168 | tf_op jit(solution)/shard_map/psum | solution.py:47
  397.2 3.1 copy.13
  (29 shorter events, 0.3 us)
Async XLA Ops:
  7.2 30.5 %copy-start = (bf16[512,1024]{1,0:T(8,128)(2,1)S(1)}, bf16[512,1024]{1,0:T(8,128)(2,1)}, u32[]{:S(2)}) copy-start(bf16[512,1024]{1,0:T(8,128)(2,1)} %param.7) | copy-start | bytes 3145732
  41.0 23.5 %all-to-all-start.1 = ((bf16[128,4,1024]{2,1,0:T(4,128)(2,1)}), bf16[128,4,1024]{2,1,0:T(4,128)(2,1)S(1)}, u32[]{:S(2)}, u32[]{:S(2)}) async-start(bf16[128,4,1024]{2,1,0:T(4,128)(2,1)} %reshape.72), calls=%async_computation.1 | async-start | bytes 2097152 | tf_op jit(solution)/shard_map/all_to_all | solution.py:23
  45.4 110.8 %all-gather.3.cloned.1.call-start = ((), (), s32[]{:S(2)}) async-start(), calls=%async_computation.4 | async-start | bytes 17825792 | tf_op jit(solution)/shard_map/all_gather | solution.py:34
  64.7 2.9 copy-start.2
  64.7 3.0 copy-start.5
  67.5 238.5 %all-reduce.3.cloned.1.call-start = ((), (), s32[]{:S(2)}) async-start(), calls=%async_computation.2 | async-start | bytes 4194304 | tf_op jit(solution)/shard_map/psum | solution.py:47
  156.2 13.5 %copy-start.1 = (bf16[4,16,128,128]{3,2,1,0:T(8,128)(2,1)S(1)}, bf16[4,16,128,128]{3,2,1,0:T(8,128)(2,1)}, u32[]{:S(2)}) copy-start(bf16[4,16,128,128]{3,2,1,0:T(8,128)(2,1)} %param.11) | copy-start | bytes 6291460
  169.7 7.3 %copy-start.3 = (bf16[1024,512]{1,0:T(8,128)(2,1)S(1)}, bf16[1024,512]{1,0:T(8,128)(2,1)}, u32[]{:S(2)}) copy-start(bf16[1024,512]{1,0:T(8,128)(2,1)} %param.12) | copy-start | bytes 3145732
  177.0 1.7 copy-start.4
  180.9 216.3 %all-reduce.5.cloned.1.call-start = ((), (), s32[]{:S(2)}) async-start(), calls=%async_computation.3 | async-start | bytes 4194304 | tf_op jit(solution)/shard_map/psum | solution.py:47
Sparse Core Ops, SparseCore 0:
  67.6 88.4 all-gather.2
  181.1 124.8 all-reduce.2
  308.5 88.6 all-reduce.4

commit v2 on v0

--- a/solution.py
+++ b/solution.py
@@ -30,7 +30,10 @@
     hidden_units = weight.shape[1]
     tiles_dev, blocks, tile_size, _ = block_vals.shape
     ordered = regroup(features, node_order)
-    everyone = lax.all_gather(ordered, "dom", axis=0, tiled=True)
+    peers = lax.axis_size("dom")
+    pieces = jnp.stack([ordered for _ in range(peers)])
+    pieces = lax.all_to_all(pieces, "dom", split_axis=0, concat_axis=0)
+    everyone = jnp.concatenate(pieces, axis=0)
     panel_tiles = everyone.reshape(-1, tile_size, width_in)
     live_mask = lax.broadcasted_iota(jnp.int32, (tiles_dev, blocks), 1) < block_count[:, None]
     masked_vals = jnp.where(live_mask[:, :, None, None], block_vals, jnp.zeros((), jnp.bfloat16))

time: 342 us -> 445 us (1.30)
  waiting for transfers between devices: 255 us -> 346 us
  starting transfers between devices: 4.48 us -> 10.6 us
  local copies, waits for them, and re-layouts: 27.2 us -> 32.6 us
    all_to_all x0 -> x1, waiting for transfers between devices: none -> 184 us  [shards(): pieces = lax.all_to_all(pieces, 'dom', split_axis=0, concat_axis=0)]
    all_gather x1 -> x0, waiting for transfers between devices: 88.4 us -> none  [shards(): everyone = lax.all_gather(ordered, 'dom', axis=0, tiled=True)]
    all_to_all x0 -> x1, starting transfers between devices: none -> 6.21 us  [shards(): pieces = lax.all_to_all(pieces, 'dom', split_axis=0, concat_axis=0)]
    another operation x0 -> x1, local copies, waits for them, and re-layouts: none -> 5.99 us  [shards(): pieces = jnp.stack([ordered for _ in range(peers)])]
    psum x1, waiting for transfers between devices: 151 us -> 146 us  [shards(): grad_weight = lax.psum(local_grad, ('grp', 'dom'))]
where the time goes in v2:
time: 445 us
  waiting for transfers between devices  346 us (78%)
  local copies, waits for them, and re-layouts  32.6 us (7%)
  blocking collectives  20.9 us (5%)
  between operations  14.2 us (3%)
  matrix products  11.2 us (3%)
  starting transfers between devices  10.6 us (2%)
  other arithmetic  9.24 us (2%)
    all_to_all x1, waiting for transfers between devices, shards(): pieces = lax.all_to_all(pieces, 'dom', split_axis=0, concat_axis=0)  184 us
    psum x1, waiting for transfers between devices, shards(): grad_weight = lax.psum(local_grad, ('grp', 'dom'))  146 us
    all_to_all x1, blocking collectives, regroup(): lax.all_to_all(requests, ('grp', 'dom'), split_axis=0, concat_axis=0, til...  20.9 us
    all_to_all x1, waiting for transfers between devices, regroup(): lax.all_to_all(outgoing, ('grp', 'dom'), split_axis=0, concat_axis=0, til...  15.3 us
    gather x1, local copies, waits for them, and re-layouts, shards(): selected = panel_tiles[block_cols]  13.5 us
  transfers between devices with their start and end apart: 3, of which 3 were waited for; matrix products, arithmetic and copies ran while one was open for 1% of the time, Pallas kernels for 0%

profile of v2, /device:TPU:1, one launch (start us, length us, event | category | flops | bytes accessed | tf_op | source)
XLA Modules:
  0.0 444.6 jit_solution(323666849598027105)
XLA Ops:
  7.2 0.8 add_select_fusion
  8.0 3.8 sort.34
  11.7 3.5 gather_fusion
  15.2 0.1 all_to_all.12
  15.4 20.9 %all_to_all.19 = s32[128,1,4]{2,1,0:T(1,128)S(1)} all-to-all(s32[128,1,4]{2,1,0:T(1,128)S(1)} %bitcast.15), channel_id=1, replica_groups=mesh['grp'=8,'dom'=16] {'grp','dom'}, dimensions={0} | all-to-all | bytes 4096 | tf_op jit(solution)/shard_map/all_to_all | solution.py:20
  36.2 0.5 broadcast.78
  36.7 0.8 reduce.3
  37.6 0.1 reshape.70
  37.7 2.1 gather_fusion.1
  39.8 1.2 reshape.71
  41.0 4.4 all-to-all-start.1
  45.4 3.8 sort.35
  49.2 15.3 %all-to-all-done.1 = bf16[128,4,1024]{2,1,0:T(4,128)(2,1)S(1)} async-done(((bf16[128,4,1024]{2,1,0:T(4,128)(2,1)}), bf16[128,4,1024]{2,1,0:T(4,128)(2,1)S(1)}, u32[]{:S(2)}, u32[]{:S(2)}) %all-to-all-start.1) | async-done | bytes 1048608 | tf_op jit(solution)/shard_map/all_to_all | solution.py:22
  64.4 0.3 reshape.72
  64.7 2.1 gather_fusion.2
  66.8 6.0 %stack.2 = bf16[16,512,1024]{2,1,0:T(8,128)(2,1)} broadcast(bf16[512,1024]{1,0:T(8,128)(2,1)S(1)} %gather_fusion.2), dimensions={1,2} | broadcast | bytes 17825792 | tf_op jit(solution)/shard_map/stack | solution.py:34
  72.8 6.2 %all-to-all-start.2 = ((bf16[16,512,1024]{2,1,0:T(8,128)(2,1)}), bf16[16,512,1024]{2,1,0:T(8,128)(2,1)}, u32[]{:S(2)}, u32[]{:S(2)}) async-start(bf16[16,512,1024]{2,1,0:T(8,128)(2,1)} %stack.2), calls=%async_computation.2 | async-start | bytes 33554432 | tf_op jit(solution)/shard_map/all_to_all | solution.py:35
  79.2 184.4 %all-to-all-done.2 = bf16[16,512,1024]{2,1,0:T(8,128)(2,1)} async-done(((bf16[16,512,1024]{2,1,0:T(8,128)(2,1)}), bf16[16,512,1024]{2,1,0:T(8,128)(2,1)}, u32[]{:S(2)}, u32[]{:S(2)}) %all-to-all-start.2) | async-done | bytes 16777248 | tf_op jit(solution)/shard_map/all_to_all | solution.py:35
  263.6 13.5 %gather_fusion.3 = bf16[64,128,1024]{2,1,0:T(8,128)(2,1)} fusion(bf16[64,128,1024]{2,1,0:T(8,128)(2,1)} %bitcast.2, s32[1024]{0:T(1024)S(1)} %pad_clamp_fusion), kind=kCustom, calls=%fused_computation.3 | custom fusion | bytes 33554688 | tf_op jit(solution)/shard_map/gather | solution.py:40
  277.1 7.3 %bitcast_convert_fusion = bf16[4,128,1024]{2,1,0:T(8,128)(2,1)S(1)} fusion(bf16[4,16,128,1024]{3,2,1,0:T(8,128)(2,1)} %bitcast.12, bf16[4,16,128,128]{3,2,1,0:T(8,128)(2,1)S(1)} %copy-done.2, pred[4,16]{1,0:T(4,128)(4,1)S(1)} %iota_compare_fusion), kind=kOutput, calls=%fused_computation.4 | convolution fusion | flops 2149056512 | bytes 19923008 | tf_op jit(solution)/shard_map/tkij,tkjf->tif/dot_general | solution.py:41
  284.5 1.6 multiply_convert_fusion.1
  286.1 2.2 fusion.6
  288.4 146.2 %all-reduce.2.cloned.1.call-done = f32[1024,512]{1,0:T(8,128)} async-done(((f32[1024,512]{1,0:T(8,128)}), f32[1024,512]{1,0:T(8,128)}) %all-reduce.2.cloned.1.call-update) | async-done | bytes 2097168 | tf_op jit(solution)/shard_map/psum | solution.py:49
  434.6 3.2 copy.12
  (28 shorter events, 0.3 us)
Async XLA Ops:
  7.2 30.5 %copy-start = (bf16[512,1024]{1,0:T(8,128)(2,1)S(1)}, bf16[512,1024]{1,0:T(8,128)(2,1)}, u32[]{:S(2)}) copy-start(bf16[512,1024]{1,0:T(8,128)(2,1)} %param.7) | copy-start | bytes 3145732
  41.0 23.5 %all-to-all-start.1 = ((bf16[128,4,1024]{2,1,0:T(4,128)(2,1)}), bf16[128,4,1024]{2,1,0:T(4,128)(2,1)S(1)}, u32[]{:S(2)}, u32[]{:S(2)}) async-start(bf16[128,4,1024]{2,1,0:T(4,128)(2,1)} %reshape.71), calls=%async_computation.1 | async-start | bytes 2097152 | tf_op jit(solution)/shard_map/all_to_all | solution.py:22
  72.8 6.3 %copy-start.3 = (s32[4,16]{1,0:T(4,128)S(1)}, s32[4,16]{1,0:T(4,128)}, u32[]{:S(2)}) copy-start(s32[4,16]{1,0:T(4,128)} %param.9) | copy-start | bytes 772
  72.8 6.4 %copy-start.6 = (s32[4]{0:T(128)S(1)}, s32[4]{0:T(128)}, u32[]{:S(2)}) copy-start(s32[4]{0:T(128)} %param.10) | copy-start | bytes 52
  72.8 190.8 %all-to-all-start.2 = ((bf16[16,512,1024]{2,1,0:T(8,128)(2,1)}), bf16[16,512,1024]{2,1,0:T(8,128)(2,1)}, u32[]{:S(2)}, u32[]{:S(2)}) async-start(bf16[16,512,1024]{2,1,0:T(8,128)(2,1)} %stack.2), calls=%async_computation.2 | async-start | bytes 33554432 | tf_op jit(solution)/shard_map/all_to_all | solution.py:35
  79.0 355.6 %all-reduce.2.cloned.1.call-start = ((), (), s32[]{:S(2)}) async-start(), calls=%async_computation.3 | async-start | bytes 4194304 | tf_op jit(solution)/shard_map/psum | solution.py:49
  263.6 13.5 %copy-start.2 = (bf16[4,16,128,128]{3,2,1,0:T(8,128)(2,1)S(1)}, bf16[4,16,128,128]{3,2,1,0:T(8,128)(2,1)}, u32[]{:S(2)}) copy-start(bf16[4,16,128,128]{3,2,1,0:T(8,128)(2,1)} %param.11) | copy-start | bytes 6291460
  277.1 7.3 %copy-start.4 = (bf16[1024,512]{1,0:T(8,128)(2,1)S(1)}, bf16[1024,512]{1,0:T(8,128)(2,1)}, u32[]{:S(2)}) copy-start(bf16[1024,512]{1,0:T(8,128)(2,1)} %param.12) | copy-start | bytes 3145732
  284.4 1.7 copy-start.5
  434.6 3.2 copy-start.1
Sparse Core Ops, SparseCore 0:
  288.5 146.0 all-reduce.1
